TPU v7x, 32 devices: a whole 2x2x4 slice. The times are simulated.
32 devices in a mesh: groups: 1, ctx: 16 (over z, y, x), tp: 2 (over core).
Axes of the slice: x: 2, y: 2, z: 4, core: 2. Of those that a mesh axis runs over, the one named last changes fastest.
Arguments:
- queries: bfloat16 [4, 32, 64, 128], P('groups', 'ctx', 'tp'), may hold values from -100 to 100
- cand_keys: bfloat16 [4, 32, 8, 128], P('groups', 'ctx', 'tp'), may hold values from -4 to 4
- candidate_values: bfloat16 [4, 32, 8, 128], P('groups', 'ctx', 'tp'), may hold values from -5 to 5
- cached_prompt_keys: bfloat16 [256, 128, 8, 128], P(('groups', 'ctx'), None, 'tp'), may hold values from -4 to 4
- cached_prompt_values: bfloat16 [256, 128, 8, 128], P(('groups', 'ctx'), None, 'tp'), may hold values from -5 to 5
- block_lists: int32 [4, 128], P('groups'), may hold values from 0 to 255, as said below
- out_weight: bfloat16 [8192, 8192], P('tp', 'ctx'), may hold values from -0.0625 to 0.0625
Outputs:
- verified: bfloat16 [4, 32, 8192], P('groups', 'tp', 'ctx')
Inputs may be any that keep to these rules, and one draw needn't show every extreme that they name: `block_lists`: each row holds 128 distinct block numbers in increasing order; among blocks 16 * c to 16 * (c + 1) - 1 a row has at most 16 entries, exactly 16 for some c in every row; all rows together have at most 40 entries in one such range, exactly 40 in some.
All inputs are finite; a program needn't handle non-finite values.
Results may differ from a plain program's by a relative error of at most 0.022.
Values may be sent and summed in bfloat16 or wider, within the bound.
A program may use at most 128 MiB of HBM per device.

v0:
```python
import functools
import math

import jax
import jax.numpy as jnp
from jax import lax
from jax.experimental import pallas as pl
from jax.experimental.pallas import tpu as pltpu
from jax.sharding import PartitionSpec as P

NEGATIVE = -1e30
MESH = pl.DeviceIdType.MESH
F32, BF16 = jnp.float32, jnp.bfloat16


class Place:
    def __init__(self, ranges):
        self.me = lax.axis_index("ctx")
        self.depth = ranges // 4
        self.x, self.y, self.z = self.me % 2, (self.me // 2) % 2, self.me // 4
        self.beside_x = self.at(self.z, self.y, 1 - self.x)
        self.beside_y = self.at(self.z, 1 - self.y, self.x)

    def at(self, z, y, x):
        return z * 4 + y * 2 + x

    def shifted(self, d):
        return (self.z + d + self.depth) % self.depth

    def line(self, d):
        return self.at(self.shifted(d), self.y, self.x)


def greet(place, with_tp):
    barrier = pltpu.get_barrier_semaphore()
    others = [place.line(d) for d in range(1, place.depth)]
    for other in others + [place.beside_x, place.beside_y]:
        pl.semaphore_signal(barrier, inc=1, device_id={"ctx": other}, device_id_type=MESH)
    if with_tp:
        pl.semaphore_signal(
            barrier, inc=1, device_id={"tp": 1 - lax.axis_index("tp")}, device_id_type=MESH
        )
    pl.semaphore_wait(barrier, place.depth + 1 + int(with_tp))


def near_first(depth):
    order = []
    for step in range(1, depth // 2 + 1):
        order += [step] + ([depth - step] if depth - step != step else [])
    return order


def gather_pieces(place, buf, send, recv, work=lambda step: None):
    def copy(kind, d, half, owner, target):
        return pltpu.make_async_remote_copy(
            src_ref=buf.at[owner, half],
            dst_ref=buf.at[owner, half],
            send_sem=send.at[kind, d, half],
            recv_sem=recv.at[kind, d, half],
            device_id={"ctx": target},
            device_id_type=MESH,
        )

    sent = []

    def go(*what):
        one = copy(*what)
        one.start()
        sent.append(one)

    depth = place.depth
    z_of = [place.shifted(-d) for d in range(depth)]

    def spread(d, half):
        owner = place.at(z_of[d], place.y, place.x)
        if d:
            copy(0, d, half, owner, place.me).wait_recv()
        go(1, d, half, owner, place.beside_x)
        go(2, d, half, owner, place.beside_y)

    def relay(d, half):
        from_x = place.at(z_of[d], place.y, 1 - place.x)
        from_y = place.at(z_of[d], 1 - place.y, place.x)
        if half == 0:
            copy(1, d, half, from_x, place.me).wait_recv()
            go(3, d, half, from_x, place.beside_y)
        else:
            copy(2, d, half, from_y, place.me).wait_recv()
            go(3, d, half, from_y, place.beside_x)

    def settle(d, half):
        from_x = place.at(z_of[d], place.y, 1 - place.x)
        from_y = place.at(z_of[d], 1 - place.y, place.x)
        if half == 0:
            copy(2, d, half, from_y, place.me).wait_recv()
        else:
            copy(1, d, half, from_x, place.me).wait_recv()
        across = place.at(z_of[d], 1 - place.y, 1 - place.x)
        copy(3, d, half, across, place.me).wait_recv()

    order = near_first(depth)
    for half in range(2):
        spread(0, half)
    for d in order:
        for half in range(2):
            go(0, d, half, place.me, place.line(d))
    work(0)
    steps = [(d, half) for d in [0] + order for half in range(2)]
    for i, step in enumerate(steps):
        if i + 2 < len(steps):
            spread(*steps[i + 2])
        relay(*step)
        work(i + 1)
    for step in steps:
        settle(*step)
    for one in sent:
        one.wait_send()


def query_kernel(
    ranges,
    kv,
    q_ref,
    k_ref,
    v_ref,
    out_ref,
    k_out,
    v_out,
    raw,
    wide,
    heads,
    send,
    recv,
    in_sems,
    out_sems,
):
    place = Place(ranges)
    sources, results = (k_ref, v_ref), (k_out, v_out)
    fetches = [pltpu.make_async_copy(sources[n], raw.at[n], in_sems.at[n]) for n in range(2)]
    for fetch in fetches:
        fetch.start()
    out_ref[place.me] = q_ref[...]
    greet(place, False)
    blocks, block_tokens = raw.shape[1], raw.shape[2] // kv
    parts = 4
    per = blocks // parts
    stores = []

    def work(step):
        if step >= 2 * parts:
            return
        n, part = step // parts, step % parts
        if part == 0:
            fetches[n].wait()

        def one(b, carry):
            wide[...] = raw[n, b].astype(F32)
            for h in range(kv):
                heads[n, h, b] = wide[pl.ds(h, block_tokens, stride=kv), :].astype(BF16)
            return carry

        lax.fori_loop(part * per, (part + 1) * per, one, 0)
        some = pl.ds(part * per, per)
        store = pltpu.make_async_copy(
            heads.at[n, :, some], results[n].at[:, some], out_sems.at[n, part]
        )
        store.start()
        stores.append(store)

    gather_pieces(place, out_ref, send, recv, work)
    for store in stores:
        store.wait()


def attend_kernel(
    sizes,
    lists_smem,
    lists_ref,
    q_ref,
    own_k_ref,
    own_v_ref,
    k_ref,
    v_ref,
    out_ref,
    k_heads,
    v_heads,
    scores,
    sums,
    acc,
    top,
    sems,
):
    cands, toks, kv, group, blocks, block_tokens, head, tile_owners = sizes
    chunk = pl.program_id(0)
    me = lax.axis_index("ctx")
    scale = head ** (-0.5) * math.log2(math.e)
    rows = tile_owners * toks * group
    lowest = me * blocks

    fetch_k = pltpu.make_async_copy(k_ref, k_heads, sems.at[0])
    fetch_v = pltpu.make_async_copy(v_ref, v_heads, sems.at[1])

    @pl.when(chunk == 0)
    def _():
        fetch_k.start()
        fetch_v.start()

    key_row = lax.broadcasted_iota(jnp.int32, (block_tokens, head), 0)

    def own_block(ref, h, j):
        rows_here = ref[j].astype(F32)
        block = jnp.zeros((block_tokens, head), F32)
        for t in range(toks):
            block = jnp.where(key_row == t, rows_here[t, h : h + 1, :], block)
        return block.astype(BF16)

    row = lax.broadcasted_iota(jnp.int32, (rows, block_tokens), 0)
    lane = lax.broadcasted_iota(jnp.int32, (rows, block_tokens), 1)
    query_pos = chunk * tile_owners * toks + row // group
    own_seen = (lane < toks) & (me * toks + lane <= query_pos)
    stats = [jnp.zeros((rows, 128), F32)] * 2
    per = toks * group
    lanes = lax.broadcasted_iota(jnp.int32, (rows, 128), 1)
    nt = (((1,), (1,)), ((), ()))
    for j in range(cands):
        line = lists_ref[j : j + 1, :]
        below = jnp.sum((line < lowest).astype(jnp.int32))
        count = jnp.sum((line < lowest + blocks).astype(jnp.int32)) - below
        last = lists_smem.shape[1] - 1

        def listed(slot):
            return lists_smem[j, jnp.minimum(below + slot, last)] - lowest

        fours = count // 4
        pairs = (count - 4 * fours + 1) // 2

        def four_of(i):
            return 4 * i, [listed(4 * i + n) for n in range(4)], None

        def pair_of(i):
            slot = 4 * fours + 2 * i
            inside = slot + 1 < count
            first = listed(slot)
            return slot, [first, jnp.where(inside, listed(slot + 1), first)], inside

        def scores_of(h, picked):
            keys = jnp.concatenate([k_heads[h, b] for b in picked], axis=0)
            s = lax.dot_general(queries[h], keys, nt, preferred_element_type=F32)
            return [s[:, n * block_tokens : (n + 1) * block_tokens] for n in range(len(picked))]

        queries = []
        for h in range(kv):
            q = q_ref[:, j, :, h * group : (h + 1) * group, :].astype(F32)
            queries.append(q.reshape(rows, head).astype(BF16))
            own = lax.dot_general(
                queries[h], own_block(own_k_ref, h, j), nt, preferred_element_type=F32
            )
            own = jnp.where(own_seen, own, NEGATIVE)
            sums[h] = own
            top[h] = own

        if j == 0:
            pl.when(chunk == 0)(fetch_k.wait)

        def first_pass(pick, i, carry):
            slot, picked, _ = pick(i)
            for h in range(kv):
                found = scores_of(h, picked)
                for n, s in enumerate(found):
                    scores[h, slot + n] = s
                top[h] = functools.reduce(jnp.maximum, found, top[h])
            return carry

        lax.fori_loop(0, fours, functools.partial(first_pass, four_of), 0)
        lax.fori_loop(0, pairs, functools.partial(first_pass, pair_of), 0)
        for h in range(kv):
            peak = jnp.max(top[h], axis=1, keepdims=True).astype(BF16).astype(F32)
            p = jnp.where(own_seen, jnp.exp2((sums[h] - peak) * scale), 0.0)
            sums[h] = p
            acc[h] = jnp.dot(
                p.astype(BF16), own_block(own_v_ref, h, j), preferred_element_type=F32
            )
            top[h] = jnp.broadcast_to(peak, (rows, block_tokens))

        def second_pass(pick, i, carry):
            slot, picked, inside = pick(i)
            for h in range(kv):
                peak = top[h]
                p = [
                    jnp.exp2((scores[h, slot + n] - peak) * scale) for n in range(len(picked))
                ]
                if inside is not None:
                    p[-1] = jnp.where(inside, p[-1], 0.0)
                sums[h] += functools.reduce(jnp.add, p)
                values = jnp.concatenate([v_heads[h, b] for b in picked], axis=0)
                weights = jnp.concatenate([one.astype(BF16) for one in p], axis=1)
                acc[h] += jnp.dot(weights, values, preferred_element_type=F32)
            return carry

        if j == 0:
            pl.when(chunk == 0)(fetch_v.wait)
        lax.fori_loop(0, fours, functools.partial(second_pass, four_of), 0)
        lax.fori_loop(0, pairs, functools.partial(second_pass, pair_of), 0)
        for h in range(kv):
            half, combo = h // (kv // 2), (h % (kv // 2)) * cands + j
            total = jnp.sum(sums[h], axis=1, keepdims=True)
            stats[half] = jnp.where(lanes == combo, top[h], stats[half])
            stats[half] = jnp.where(lanes == 64 + combo, total, stats[half])
            out_ref[:, half, combo * per : (combo + 1) * per, :] = (
                acc[h].reshape(tile_owners, per, head).astype(BF16)
            )
    full = kv // 2 * cands * per
    for half in range(2):
        out_ref[:, half, full : full + per, :] = (
            stats[half].reshape(tile_owners, per, 128).astype(BF16)
        )


def merge(pieces, combos, per, scale):
    full = combos * per
    stats = [load(full, per).astype(F32) for load in pieces]
    peak = functools.reduce(jnp.maximum, stats)
    low = lax.broadcasted_iota(jnp.int32, (per, 128), 1) < 64
    scales = [jnp.exp2((jnp.where(low, s - peak, 0.0)) * scale) for s in stats]
    total = sum(pltpu.roll(w, 64, 1) * s for w, s in zip(scales, stats))
    sums = []
    for c in range(combos):
        sums.append(
            sum(
                load(c * per, per).astype(F32) * w[:, c : c + 1]
                for load, w in zip(pieces, scales)
            )
        )
    return sums, jnp.where(low, peak, total), total


def finish_kernel(
    ranges,
    sizes,
    parts_ref,
    weight_ref,
    out_ref,
    from_diag,
    from_x,
    from_y,
    from_line,
    to_diag,
    to_line,
    gathered,
    ordered,
    weight,
    total,
    away,
    arrived,
    lines,
    weight_sem,
    red_send,
    red_recv,
    send,
    recv,
    tp_sems,
):
    cands, toks, kv, group, head = sizes
    place = Place(ranges)
    depth = place.depth
    per = toks * group
    combos = kv // 2 * cands
    scale = head ** (-0.5) * math.log2(math.e)
    fetch = pltpu.make_async_copy(weight_ref, weight, weight_sem)
    fetch.start()
    greet(place, True)

    sent = []

    def copy(kind, d, half, src, dst, target):
        return pltpu.make_async_remote_copy(
            src_ref=src,
            dst_ref=dst.at[d, half],
            send_sem=red_send.at[kind, d, half],
            recv_sem=red_recv.at[kind, d, half],
            device_id={"ctx": target},
            device_id_type=MESH,
        )

    def go(*what):
        one = copy(*what)
        one.start()
        sent.append(one)

    def arrive(kind, d, half, dst):
        copy(kind, d, half, dst.at[d, half], dst, place.me).wait_recv()

    def owner(d, flip_y, flip_x):
        y = 1 - place.y if flip_y else place.y
        x = 1 - place.x if flip_x else place.x
        return place.at(place.shifted(d), y, x)

    def loader(ref, *index):
        return lambda start, size: ref[(*index, pl.ds(start, size), slice(None))]

    def put(dst, d, half, sums, stats):
        for c in range(combos):
            dst[d, half, c * per : (c + 1) * per, :] = sums[c].astype(BF16)
        dst[d, half, combos * per : (combos + 1) * per, :] = stats.astype(BF16)

    def begin(d):
        go(0, d, 0, parts_ref.at[owner(d, 1, 1), 0], from_diag, place.beside_x)
        go(0, d, 1, parts_ref.at[owner(d, 1, 1), 1], from_diag, place.beside_y)
        go(1, d, 0, parts_ref.at[owner(d, 0, 1), 0], from_x, place.beside_x)
        go(2, d, 1, parts_ref.at[owner(d, 1, 0), 1], from_y, place.beside_y)

    def pass_on(d):
        for half in range(2):
            arrive(0, d, half, from_diag)
            mine = owner(d, 1, 0) if half == 0 else owner(d, 0, 1)
            pieces = (loader(parts_ref, mine, half), loader(from_diag, d, half))
            sums, stats, _ = merge(pieces, combos, per, scale)
            put(to_diag, d, half, sums, stats)
            if half == 0:
                go(2, d, half, to_diag.at[d, half], from_y, place.beside_y)
            else:
                go(1, d, half, to_diag.at[d, half], from_x, place.beside_x)

    def plane(d):
        for half in range(2):
            arrive(1, d, half, from_x)
            arrive(2, d, half, from_y)
            pieces = (
                loader(parts_ref, owner(d, 0, 0), half),
                loader(from_x, d, half),
                loader(from_y, d, half),
            )
            sums, stats, _ = merge(pieces, combos, per, scale)
            put(to_line, d, half, sums, stats)
            if d:
                go(3, d, half, to_line.at[d, half], from_line, place.line(d))

    order = near_first(depth)[::-1] + [0]
    begin(order[0])
    begin(order[1])
    for i, d in enumerate(order):
        pass_on(d)
        if i + 2 < depth:
            begin(order[i + 2])
        if i >= 1:
            plane(order[i - 1])
    plane(order[-1])
    for half in range(2):
        for d in range(1, depth):
            arrive(3, d, half, from_line)
        sums, _, denominator = merge(
            [loader(to_line, 0, half)] + [loader(from_line, d, half) for d in range(1, depth)],
            combos,
            per,
            scale,
        )
        denominator = pltpu.roll(denominator, 64, 1)
        for c in range(combos):
            row = (half * combos + c) * per
            ordered[row : row + per, :] = sums[c] / denominator[:, c : c + 1]
    tokens = cands * toks
    for h in range(kv):
        block = [
            ordered[pl.ds(h * tokens * group + g, tokens, stride=group), :] for g in range(group)
        ]
        half, at = h // (kv // 2), (h % (kv // 2)) * tokens * group
        gathered[place.me, half, at : at + tokens * group, :] = jnp.concatenate(
            block, axis=0
        ).astype(BF16)
    gather_pieces(place, gathered, send, recv)
    fetch.wait()
    total[...] = jnp.zeros_like(total)

    def project(i, carry):
        steps = kv * group // 4
        start = pl.multiple_of((i % steps) * 2 * tokens, 2 * tokens)
        both = gathered[:, i // steps, pl.ds(start, 2 * tokens), :].astype(F32)
        left = both[:, :tokens, :].reshape(ranges * tokens, head).astype(BF16)
        right = both[:, tokens:, :].reshape(ranges * tokens, head).astype(BF16)
        rows = pl.multiple_of(i * 2 * head, 2 * head)
        total[...] += jnp.dot(
            jnp.concatenate([left, right], axis=1),
            weight[pl.ds(rows, 2 * head), :],
            preferred_element_type=F32,
        )
        return carry

    lax.fori_loop(0, kv * group // 2, project, 0)
    half = ranges * tokens // 2
    tp = lax.axis_index("tp")
    away[...] = total[pl.ds(pl.multiple_of((1 - tp) * half, half), half), :].astype(BF16)
    swap = pltpu.make_async_remote_copy(
        src_ref=away,
        dst_ref=arrived,
        send_sem=tp_sems.at[0],
        recv_sem=tp_sems.at[1],
        device_id={"tp": 1 - tp},
        device_id_type=MESH,
    )
    swap.start()
    for one in sent:
        one.wait_send()
    swap.wait()
    mine = total[pl.ds(pl.multiple_of(tp * half, half), half), :]
    columns = total.shape[1]
    joined = mine + arrived[...].astype(F32)
    owners, size = ranges // 2, ranges // 2 * toks
    for c in range(columns // 128):
        lines[c, 0] = joined[:, c * 128 : (c + 1) * 128]
        for j in range(cands):
            for t in range(toks):
                lines[c, 1, pl.ds(j * size + t, owners, stride=toks), :] = lines[
                    c, 0, pl.ds(j * toks + t, owners, stride=tokens), :
                ]
            out_ref[j, :, c * 128 : (c + 1) * 128] = lines[
                c, 1, j * size : (j + 1) * size, :
            ].astype(BF16)


def on_device(
    queries,
    cand_keys,
    candidate_values,
    cached_prompt_keys,
    cached_prompt_values,
    block_lists,
    out_weight,
):
    cands, toks, heads, head = queries.shape
    kv = cand_keys.shape[2]
    group = heads // kv
    blocks, block_tokens = cached_prompt_keys.shape[:2]
    ranges = lax.axis_size("ctx")
    depth = ranges // 4
    piece = cands * toks * heads
    per = toks * group
    vmem = pl.BlockSpec(memory_space=pltpu.VMEM)
    limit = 60 * 1024 * 1024

    anywhere = pl.BlockSpec(memory_space=pl.ANY)
    semaphores = [pltpu.SemaphoreType.DMA((4, depth, 2))] * 2
    cache = (blocks, block_tokens * kv, head)
    sorted_cache = (kv, blocks, block_tokens, head)
    everyone, keys, values = pl.pallas_call(
        functools.partial(query_kernel, ranges, kv),
        out_shape=(
            jax.ShapeDtypeStruct((ranges, 2, piece // 2, head), BF16),
            jax.ShapeDtypeStruct(sorted_cache, BF16),
            jax.ShapeDtypeStruct(sorted_cache, BF16),
        ),
        in_specs=[vmem, anywhere, anywhere],
        out_specs=(vmem, anywhere, anywhere),
        scratch_shapes=[
            pltpu.VMEM((2, *cache), BF16),
            pltpu.VMEM((block_tokens * kv, head), F32),
            pltpu.VMEM((2, *sorted_cache), BF16),
            *semaphores,
            pltpu.SemaphoreType.DMA((2,)),
            pltpu.SemaphoreType.DMA((2, 4)),
        ],
        compiler_params=pltpu.CompilerParams(
            collective_id=0, has_side_effects=True, vmem_limit_bytes=limit
        ),
        name="query_gather",
    )(
        queries.reshape(2, piece // 2, head),
        cached_prompt_keys.reshape(cache),
        cached_prompt_values.reshape(cache),
    )

    tile_owners = min(ranges, 256 // per)
    rows = tile_owners * per
    half_rows = piece // 2 + per
    whole = lambda shape: pl.BlockSpec(
        shape, lambda i, *_: (0,) * len(shape), pipeline_mode=pl.Buffered(1)
    )
    own_spec = whole(cand_keys.shape)
    sizes = (cands, toks, kv, group, blocks, block_tokens, head, tile_owners)
    parts = pl.pallas_call(
        functools.partial(attend_kernel, sizes),
        out_shape=jax.ShapeDtypeStruct((ranges, 2, half_rows, head), BF16),
        grid_spec=pltpu.PrefetchScalarGridSpec(
            num_scalar_prefetch=1,
            grid=(ranges // tile_owners,),
            in_specs=[
                whole(block_lists.shape),
                pl.BlockSpec(
                    (tile_owners, cands, toks, heads, head), lambda i, *_: (i, 0, 0, 0, 0)
                ),
                own_spec,
                own_spec,
                anywhere,
                anywhere,
            ],
            out_specs=pl.BlockSpec((tile_owners, 2, half_rows, head), lambda i, *_: (i, 0, 0, 0)),
            scratch_shapes=[
                pltpu.VMEM((kv, blocks, block_tokens, head), BF16),
                pltpu.VMEM((kv, blocks, block_tokens, head), BF16),
                pltpu.VMEM((kv, (blocks + 1) // 2 * 2, rows, block_tokens), F32),
                pltpu.VMEM((kv, rows, block_tokens), F32),
                pltpu.VMEM((kv, rows, head), F32),
                pltpu.VMEM((kv, rows, block_tokens), F32),
                pltpu.SemaphoreType.DMA((2,)),
            ],
        ),
        compiler_params=pltpu.CompilerParams(vmem_limit_bytes=limit),
        name="attend",
    )(
        block_lists,
        block_lists,
        everyone.reshape(ranges, cands, toks, heads, head),
        cand_keys,
        candidate_values,
        keys,
        values,
    )

    columns = out_weight.shape[1]
    tokens = cands * toks
    half = ranges * tokens // 2
    block = pltpu.VMEM((depth, 2, half_rows, head), BF16)
    return pl.pallas_call(
        functools.partial(finish_kernel, ranges, (cands, toks, kv, group, head)),
        out_shape=jax.ShapeDtypeStruct((cands, ranges * toks // 2, columns), BF16),
        in_specs=[vmem, pl.BlockSpec(memory_space=pl.ANY)],
        out_specs=vmem,
        scratch_shapes=[block] * 6
        + [
            pltpu.VMEM((ranges, 2, piece // 2, head), BF16),
            pltpu.VMEM((piece, head), F32),
            pltpu.VMEM(out_weight.shape, BF16),
            pltpu.VMEM((2 * half, columns), F32),
            pltpu.VMEM((half, columns), BF16),
            pltpu.VMEM((half, columns), BF16),
            pltpu.VMEM((columns // 128, 2, half, 128), F32),
            pltpu.SemaphoreType.DMA,
            *semaphores,
            *semaphores,
            pltpu.SemaphoreType.DMA((2,)),
        ],
        compiler_params=pltpu.CompilerParams(
            collective_id=1, has_side_effects=True, vmem_limit_bytes=limit
        ),
        name="reduce_project",
    )(parts, out_weight)


def solution(mesh):
    placed = (
        P("groups", "ctx", "tp", None),
        P("groups", "ctx", "tp", None),
        P("groups", "ctx", "tp", None),
        P(("groups", "ctx"), None, "tp", None),
        P(("groups", "ctx"), None, "tp", None),
        P("groups", None),
        P("tp", "ctx"),
    )
    return jax.shard_map(
        on_device, mesh=mesh, in_specs=placed, out_specs=P("groups", "tp", "ctx"), check_vma=False
    )
```

profile of v0, /device:TPU:0, one launch (start us, length us, event | category | flops | bytes accessed | tf_op | source)
XLA Modules:
  0.0 78.4 jit_solution(9955167445082672464)
XLA Ops:
  0.0 23.3 %query_gather.1 = (bf16[16,2,128,128]{3,2,1,0:T(8,128)(2,1)}, bf16[4,16,128,128]{3,2,1,0:T(8,128)(2,1)}, bf16[4,16,128,128]{3,2,1,0:T(8,128)(2,1)}) custom-call(bf16[2,128,128]{2,1,0:T(8,128)(2,1)} %bitcast.7, bf16[16,512,128]{2,1,0:T(8,128)(2,1)} %bitcast.4, bf16[16,512,128]{2,1,0:T(8,128)(2,1)} %bitcast.5), custom_call_target="tpu_custom_call" | custom-call | tf_op jit(solution)/shard_map/query_gather/pallas_call | solution.py:544
  23.3 15.3 %attend.1.parts_ref = bf16[16,2,144,128]{3,2,1,0:T(8,128)(2,1)} custom-call(s32[4,128]{1,0:T(4,128)} %lists_ref.1, s32[4,128]{1,0:T(4,128)} %lists_ref.1, bf16[16,4,2,32,128]{4,3,2,1,0:T(8,128)(2,1)} %bitcast.6, bf16[4,2,4,128]{3,2,1,0:T(4,128)(2,1)} %own_k_ref.1, bf16[4,2,4,128]{3,2,1,0:T(4,128)(2,1)} %own_v_ref.1, ...), custom_call_target="tpu_custom_call" | custom-call | tf_op jit(solution)/shard_map/attend/pallas_call | solution.py:579
  38.6 38.3 %reduce_project.1 = bf16[4,16,512]{2,1,0:T(8,128)(2,1)} custom-call(bf16[16,2,144,128]{3,2,1,0:T(8,128)(2,1)} %attend.1.parts_ref, bf16[4096,512]{1,0:T(8,128)(2,1)} %weight_ref.1), custom_call_target="tpu_custom_call" | custom-call | tf_op jit(solution)/shard_map/reduce_project/pallas_call | solution.py:622
  76.9 1.5 %copy.9 = bf16[4,16,512]{2,1,0:T(8,128)(2,1)} copy(bf16[4,16,512]{2,1,0:T(8,128)(2,1)} %reduce_project.1) | data formatting | bytes 131072
where the time goes:
time: 79.3 us; the launch traced here: 78.4 us
  Pallas kernels  76.9 us (97%)
  local copies, waits for them, and re-layouts  1.47 us (2%)
    pallas_call x1, Pallas kernels, on_device(): pl.pallas_call(functools.partial(finish_kernel, ranges, (cands, toks, kv,...  38.3 us
    pallas_call x1, Pallas kernels, on_device(): pl.pallas_call(functools.partial(query_kernel, ranges, kv), out_shape=(ja...  23.3 us
    pallas_call x1, Pallas kernels, on_device(): pl.pallas_call(functools.partial(attend_kernel, sizes), out_shape=jax.Sha...  15.3 us

commit v1 on v0

v1 whole, which is shorter than its diff:
```python
import functools
import math

import jax
import jax.numpy as jnp
from jax import lax
from jax.experimental import pallas as pl
from jax.experimental.pallas import tpu as pltpu
from jax.sharding import PartitionSpec as P

NEGATIVE = -1e30
MESH = pl.DeviceIdType.MESH
F32, BF16 = jnp.float32, jnp.bfloat16


class Place:
    def __init__(self, ranges):
        self.me = lax.axis_index("ctx")
        self.depth = ranges // 4
        self.x, self.y, self.z = self.me % 2, (self.me // 2) % 2, self.me // 4
        self.beside_x = self.at(self.z, self.y, 1 - self.x)
        self.beside_y = self.at(self.z, 1 - self.y, self.x)

    def at(self, z, y, x):
        return z * 4 + y * 2 + x

    def shifted(self, d):
        return (self.z + d + self.depth) % self.depth

    def line(self, d):
        return self.at(self.shifted(d), self.y, self.x)


def greet(place, with_tp):
    barrier = pltpu.get_barrier_semaphore()
    others = [place.line(d) for d in range(1, place.depth)]
    for other in others + [place.beside_x, place.beside_y]:
        pl.semaphore_signal(barrier, inc=1, device_id={"ctx": other}, device_id_type=MESH)
    if with_tp:
        pl.semaphore_signal(
            barrier, inc=1, device_id={"tp": 1 - lax.axis_index("tp")}, device_id_type=MESH
        )
    pl.semaphore_wait(barrier, place.depth + 1 + int(with_tp))


def near_first(depth):
    order = []
    for step in range(1, depth // 2 + 1):
        order += [step] + ([depth - step] if depth - step != step else [])
    return order


def merge(pieces, combos, per, scale):
    full = combos * per
    stats = [load(full, per).astype(F32) for load in pieces]
    peak = functools.reduce(jnp.maximum, stats)
    low = lax.broadcasted_iota(jnp.int32, (per, 128), 1) < 64
    scales = [jnp.exp2((jnp.where(low, s - peak, 0.0)) * scale) for s in stats]
    total = sum(pltpu.roll(w, 64, 1) * s for w, s in zip(scales, stats))
    sums = []
    for c in range(combos):
        sums.append(
            sum(
                load(c * per, per).astype(F32) * w[:, c : c + 1]
                for load, w in zip(pieces, scales)
            )
        )
    return sums, jnp.where(low, peak, total), total


class Gather:
    def __init__(self, place, buf, send, recv):
        self.place, self.buf, self.send, self.recv = place, buf, send, recv
        self.sent = []
        self.z_of = [place.shifted(-d) for d in range(place.depth)]

    def copy(self, kind, d, half, owner, target):
        return pltpu.make_async_remote_copy(
            src_ref=self.buf.at[owner, half],
            dst_ref=self.buf.at[owner, half],
            send_sem=self.send.at[kind, d, half],
            recv_sem=self.recv.at[kind, d, half],
            device_id={"ctx": target},
            device_id_type=MESH,
        )

    def go(self, *what):
        one = self.copy(*what)
        one.start()
        self.sent.append(one)

    def begin(self, half):
        place = self.place
        self.spread(0, half)
        for d in near_first(place.depth):
            self.go(0, d, half, place.me, place.line(d))

    def spread(self, d, half):
        place = self.place
        owner = place.at(self.z_of[d], place.y, place.x)
        if d:
            self.copy(0, d, half, owner, place.me).wait_recv()
        self.go(1, d, half, owner, place.beside_x)
        self.go(2, d, half, owner, place.beside_y)

    def relay(self, d, half):
        place = self.place
        if half == 0:
            from_x = place.at(self.z_of[d], place.y, 1 - place.x)
            self.copy(1, d, half, from_x, place.me).wait_recv()
            self.go(3, d, half, from_x, place.beside_y)
        else:
            from_y = place.at(self.z_of[d], 1 - place.y, place.x)
            self.copy(2, d, half, from_y, place.me).wait_recv()
            self.go(3, d, half, from_y, place.beside_x)

    def settle(self, half):
        place = self.place
        for d in range(place.depth):
            from_x = place.at(self.z_of[d], place.y, 1 - place.x)
            from_y = place.at(self.z_of[d], 1 - place.y, place.x)
            if half == 0:
                self.copy(2, d, half, from_y, place.me).wait_recv()
            else:
                self.copy(1, d, half, from_x, place.me).wait_recv()
            across = place.at(self.z_of[d], 1 - place.y, 1 - place.x)
            self.copy(3, d, half, across, place.me).wait_recv()

    def finish(self):
        for one in self.sent:
            one.wait_send()


def run_all(steps):
    for step in steps:
        step()


def weave(first, second):
    keyed = [((i + 0.5) / len(first), 0, i, step) for i, step in enumerate(first)]
    keyed += [((i + 0.5) / len(second), 1, i, step) for i, step in enumerate(second)]
    return [item[3] for item in sorted(keyed, key=lambda item: item[:3])]


def fused_kernel(
    ranges,
    sizes,
    lists_smem,
    lists_ref,
    q_ref,
    own_k_ref,
    own_v_ref,
    k_ref,
    v_ref,
    weight_ref,
    out_ref,
    everyone,
    raw,
    wide,
    heads,
    plan,
    queries,
    own_blocks,
    scores,
    run,
    acc,
    peaks,
    own_sums,
    own_acc,
    parts_ref,
    from_diag,
    from_x,
    from_y,
    from_line,
    to_diag,
    to_line,
    gathered,
    ordered,
    weight,
    total,
    away,
    arrived,
    lines,
    in_sems,
    ask_send,
    ask_recv,
    red_send,
    red_recv,
    send,
    recv,
    tp_sems,
):
    cands, toks, kv, group, head, tile_owners, slots = sizes
    place = Place(ranges)
    depth = place.depth
    per = toks * group
    pair = kv // 2
    combos = pair * cands
    scale = head ** (-0.5) * math.log2(math.e)
    rows = tile_owners * per
    blocks, block_tokens = raw.shape[1], raw.shape[2] // kv
    sources = (k_ref, v_ref)
    fetches = [pltpu.make_async_copy(sources[n], raw.at[n], in_sems.at[n]) for n in range(2)]
    for fetch in fetches:
        fetch.start()
    weight_fetch = pltpu.make_async_copy(weight_ref, weight, in_sems.at[2])
    weight_fetch.start()
    for half in range(2):
        everyone[place.me, half] = q_ref[:, :, half * pair * group : (half + 1) * pair * group, :]
    greet(place, True)

    ask = Gather(place, everyone, ask_send, ask_recv)
    near = near_first(depth)
    ask.begin(0)
    ask.begin(1)

    lowest = place.me * blocks
    listed = lists_smem.shape[1]
    below, count, start = [], [], [jnp.int32(0)]
    for j in range(cands):
        line = lists_ref[j : j + 1, :]
        below.append(jnp.sum((line < lowest).astype(jnp.int32)))
        count.append(jnp.sum((line < lowest + blocks).astype(jnp.int32)) - below[j])
        start.append(jnp.minimum(start[j] + (count[j] + 1) // 2, slots))

    def plan_slot(i, carry):
        cand, begun, under, many = jnp.int32(0), jnp.int32(0), below[0], count[0]
        for j in range(1, cands):
            here = i >= start[j]
            cand = jnp.where(here, j, cand)
            begun = jnp.where(here, start[j], begun)
            under = jnp.where(here, below[j], under)
            many = jnp.where(here, count[j], many)
        offset = 2 * (i - begun)
        plan[0, i] = cand
        for n in range(2):
            entry = jnp.minimum(under + offset + n, listed - 1)
            block = lists_smem[cand, entry] - lowest
            plan[1 + n, i] = jnp.minimum(jnp.maximum(block, 0), blocks - 1)
            plan[3 + n, i] = (offset + n < many).astype(jnp.int32)
        plan[5, i] = (offset == 0).astype(jnp.int32)
        return carry

    lax.fori_loop(0, slots, plan_slot, 0)

    def sort_heads(n, first, last):
        def one(b, carry):
            wide[...] = raw[n, b].astype(F32)
            for h in range(kv):
                heads[n, h, b] = wide[pl.ds(h, block_tokens, stride=kv), :].astype(BF16)
            return carry

        lax.fori_loop(first, last, one, 0)

    key_row = lax.broadcasted_iota(jnp.int32, (block_tokens, head), 0)

    def own_rows():
        for n, ref in enumerate((own_k_ref, own_v_ref)):
            mine = [ref[j].astype(F32) for j in range(cands)]
            for h in range(kv):
                block = jnp.zeros((block_tokens, head), F32)
                for j in range(cands):
                    for t in range(toks):
                        block = jnp.where(
                            key_row == j * toks + t, mine[j][t, h : h + 1, :], block
                        )
                own_blocks[n, h] = block.astype(BF16)

    def sort_step(n, part):
        def step():
            if part == 0:
                fetches[n].wait()
            sort_heads(n, part * (blocks // 4), (part + 1) * (blocks // 4))

        return step

    def ask_steps(gather):
        steps = []
        pieces = [(d, half) for half in range(2) for d in [0] + near]
        spreads = [piece for piece in pieces if piece[0]]
        for i, piece in enumerate(pieces):
            ahead = spreads[2 * i : 2 * i + 2] if i == 0 else spreads[i + 1 : i + 2]
            for other in ahead:
                steps.append(functools.partial(gather.spread, *other))
            steps.append(functools.partial(gather.relay, *piece))
        return steps

    local = [sort_step(0, part) for part in range(4)] + [own_rows]
    local += [sort_step(1, part) for part in range(4)]
    run_all(weave(local, ask_steps(ask)))

    nt = (((1,), (1,)), ((), ()))
    row = lax.broadcasted_iota(jnp.int32, (rows, block_tokens), 0)
    lane = lax.broadcasted_iota(jnp.int32, (rows, block_tokens), 1)
    unroll = 2

    def attend(half, tile, between):
        owners = pl.ds(tile * tile_owners, tile_owners)
        query_pos = tile * tile_owners * toks + row // group

        def own_seen(j):
            t = lane - j * toks
            return (t >= 0) & (t < toks) & (place.me * toks + t <= query_pos)

        for hh in range(pair):
            run[hh, 0] = jnp.full((rows, block_tokens), NEGATIVE, F32)
            acc[hh, 0] = jnp.zeros((rows, head), F32)
            for j in range(cands):
                q = everyone[owners, half, j, :, hh * group : (hh + 1) * group, :].astype(F32)
                queries[hh, j] = q.reshape(rows, head).astype(BF16)

        def first_pass(it, carry):
            for u in range(unroll):
                i = it * unroll + u
                cand, fresh = plan[0, i], plan[5, i] > 0
                for hh in range(pair):
                    h = half * pair + hh
                    keys = jnp.concatenate(
                        [heads[0, h, plan[1, i]], heads[0, h, plan[2, i]]], axis=0
                    )
                    s = lax.dot_general(queries[hh, cand], keys, nt, preferred_element_type=F32)
                    top = jnp.where(fresh, NEGATIVE, run[hh, i])
                    for n in range(2):
                        one = s[:, n * block_tokens : (n + 1) * block_tokens]
                        one = jnp.where(plan[3 + n, i] > 0, one, NEGATIVE)
                        scores[hh, i, n] = one
                        top = jnp.maximum(top, one)
                    run[hh, i + 1] = top
            return carry

        lax.fori_loop(0, slots // unroll, first_pass, 0)
        between[0]()
        for hh in range(pair):
            h = half * pair + hh
            for j in range(cands):
                seen = own_seen(j)
                own = lax.dot_general(
                    queries[hh, j], own_blocks[0, h], nt, preferred_element_type=F32
                )
                own = jnp.where(seen, own, NEGATIVE)
                top = jnp.where(count[j] > 0, run[hh, start[j + 1]], NEGATIVE)
                top = jnp.maximum(top, own)
                peak = jnp.max(top, axis=1, keepdims=True).astype(BF16).astype(F32)
                p = jnp.where(seen, jnp.exp2((own - peak) * scale), 0.0)
                own_sums[hh, j] = p
                own_acc[hh, j] = jnp.dot(
                    p.astype(BF16), own_blocks[1, h], preferred_element_type=F32
                )
                peaks[hh, j] = jnp.broadcast_to(peak, (rows, block_tokens))

        def second_pass(it, carry):
            for u in range(unroll):
                i = it * unroll + u
                cand, fresh = plan[0, i], plan[5, i] > 0
                for hh in range(pair):
                    h = half * pair + hh
                    peak = peaks[hh, cand]
                    p = [jnp.exp2((scores[hh, i, n] - peak) * scale) for n in range(2)]
                    run[hh, i + 1] = jnp.where(fresh, 0.0, run[hh, i]) + (p[0] + p[1])
                    values = jnp.concatenate(
                        [heads[1, h, plan[1, i]], heads[1, h, plan[2, i]]], axis=0
                    )
                    weights = jnp.concatenate([one.astype(BF16) for one in p], axis=1)
                    acc[hh, i + 1] = jnp.where(fresh, 0.0, acc[hh, i]) + jnp.dot(
                        weights, values, preferred_element_type=F32
                    )
            return carry

        lax.fori_loop(0, slots // unroll, second_pass, 0)
        between[1]()
        lanes = lax.broadcasted_iota(jnp.int32, (rows, 128), 1)
        stats = jnp.zeros((rows, 128), F32)
        for hh in range(pair):
            for j in range(cands):
                combo = hh * cands + j
                last, some = start[j + 1], count[j] > 0
                sums = jnp.where(some, run[hh, last], 0.0) + own_sums[hh, j]
                found = jnp.where(some, acc[hh, last], 0.0) + own_acc[hh, j]
                stats = jnp.where(lanes == combo, peaks[hh, j], stats)
                stats = jnp.where(
                    lanes == 64 + combo, jnp.sum(sums, axis=1, keepdims=True), stats
                )
                parts_ref[owners, half, combo * per : (combo + 1) * per, :] = found.reshape(
                    tile_owners, per, head
                ).astype(BF16)
        parts_ref[owners, half, combos * per : (combos + 1) * per, :] = stats.reshape(
            tile_owners, per, 128
        ).astype(BF16)

    sent = []

    def copy(kind, d, half, src, dst, target):
        return pltpu.make_async_remote_copy(
            src_ref=src,
            dst_ref=dst.at[d, half],
            send_sem=red_send.at[kind, d, half],
            recv_sem=red_recv.at[kind, d, half],
            device_id={"ctx": target},
            device_id_type=MESH,
        )

    def go(*what):
        one = copy(*what)
        one.start()
        sent.append(one)

    def arrive(kind, d, half, dst):
        copy(kind, d, half, dst.at[d, half], dst, place.me).wait_recv()

    def owner(d, flip_y, flip_x):
        y = 1 - place.y if flip_y else place.y
        x = 1 - place.x if flip_x else place.x
        return place.at(place.shifted(d), y, x)

    def loader(ref, *index):
        return lambda start, size: ref[(*index, pl.ds(start, size), slice(None))]

    def put(dst, d, half, sums, stats):
        for c in range(combos):
            dst[d, half, c * per : (c + 1) * per, :] = sums[c].astype(BF16)
        dst[d, half, combos * per : (combos + 1) * per, :] = stats.astype(BF16)

    def hand_over(d, half):
        across = parts_ref.at[owner(d, 1, 1), half]
        if half == 0:
            go(0, d, half, across, from_diag, place.beside_x)
        else:
            go(0, d, half, across, from_diag, place.beside_y)

    def hand_beside(d, half):
        if half == 0:
            go(1, d, half, parts_ref.at[owner(d, 0, 1), half], from_x, place.beside_x)
        else:
            go(2, d, half, parts_ref.at[owner(d, 1, 0), half], from_y, place.beside_y)

    def pass_on(d, half):
        arrive(0, d, half, from_diag)
        mine = owner(d, 1, 0) if half == 0 else owner(d, 0, 1)
        pieces = (loader(parts_ref, mine, half), loader(from_diag, d, half))
        sums, stats, _ = merge(pieces, combos, per, scale)
        put(to_diag, d, half, sums, stats)
        if half == 0:
            go(2, d, half, to_diag.at[d, half], from_y, place.beside_y)
        else:
            go(1, d, half, to_diag.at[d, half], from_x, place.beside_x)

    def plane(d, half):
        arrive(1, d, half, from_x)
        arrive(2, d, half, from_y)
        pieces = (
            loader(parts_ref, owner(d, 0, 0), half),
            loader(from_x, d, half),
            loader(from_y, d, half),
        )
        sums, stats, _ = merge(pieces, combos, per, scale)
        put(to_line, d, half, sums, stats)
        if d:
            go(3, d, half, to_line.at[d, half], from_line, place.line(d))

    far = near[::-1] + [0]

    def hand_all(half):
        for d in far:
            hand_over(d, half)
            hand_beside(d, half)

    tokens = cands * toks

    def conclude(half):
        for d in range(1, depth):
            arrive(3, d, half, from_line)
        sums, _, denominator = merge(
            [loader(to_line, 0, half)] + [loader(from_line, d, half) for d in range(1, depth)],
            combos,
            per,
            scale,
        )
        denominator = pltpu.roll(denominator, 64, 1)
        for c in range(combos):
            at = (half * combos + c) * per
            ordered[at : at + per, :] = sums[c] / denominator[:, c : c + 1]
        for hh in range(pair):
            h = half * pair + hh
            block = [
                ordered[pl.ds(h * tokens * group + g, tokens, stride=group), :]
                for g in range(group)
            ]
            at = hh * tokens * group
            gathered[place.me, half, at : at + tokens * group, :] = jnp.concatenate(
                block, axis=0
            ).astype(BF16)

    tell = Gather(place, gathered, send, recv)

    def project(i, carry):
        steps = kv * group // 4
        start_row = pl.multiple_of((i % steps) * 2 * tokens, 2 * tokens)
        both = gathered[:, i // steps, pl.ds(start_row, 2 * tokens), :].astype(F32)
        left = both[:, :tokens, :].reshape(ranges * tokens, head).astype(BF16)
        right = both[:, tokens:, :].reshape(ranges * tokens, head).astype(BF16)
        rows_at = pl.multiple_of(i * 2 * head, 2 * head)
        total[...] += jnp.dot(
            jnp.concatenate([left, right], axis=1),
            weight[pl.ds(rows_at, 2 * head), :],
            preferred_element_type=F32,
        )
        return carry

    part = functools.partial
    nothing = lambda: None
    tiles = ranges // tile_owners

    def attend_all(half, first, second):
        for tile in range(tiles):
            last = tile == tiles - 1
            attend(half, tile, (first if last else nothing, second if last else nothing))

    ask.settle(0)
    attend_all(0, nothing, nothing)
    hand_all(0)
    ask.settle(1)
    early = depth // 2
    attend_all(
        1,
        lambda: run_all([part(pass_on, d, 0) for d in far[:early]]),
        lambda: run_all(
            [part(pass_on, d, 0) for d in far[early:]] + [part(plane, d, 0) for d in far[:early]]
        ),
    )
    hand_all(1)
    run_all([part(plane, d, 0) for d in far[early:]])
    conclude(0)
    tell.begin(0)
    reduce_one = [part(pass_on, d, 1) for d in far[:2]]
    for i, d in enumerate(far):
        if i + 2 < depth:
            reduce_one.append(part(pass_on, far[i + 2], 1))
        reduce_one.append(part(plane, d, 1))
    spread_zero = [part(tell.spread, d, 0) for d in near]
    relay_zero = [part(tell.relay, d, 0) for d in [0] + near]
    tell_zero = spread_zero[:2] + relay_zero[:1]
    for i in range(2, len(near)):
        tell_zero += [spread_zero[i], relay_zero[i - 1]]
    tell_zero += relay_zero[len(near) - 1 :]
    run_all(weave(reduce_one, tell_zero))
    conclude(1)
    tell.begin(1)
    total[...] = jnp.zeros_like(total)
    tell.settle(0)
    weight_fetch.wait()
    count_half = kv * group // 4
    lax.fori_loop(0, count_half, project, 0)
    for i, d in enumerate([0] + near):
        for other in near[:2] if i == 0 else near[i + 1 : i + 2]:
            tell.spread(other, 1)
        tell.relay(d, 1)
    tell.settle(1)
    lax.fori_loop(count_half, 2 * count_half, project, 0)
    half_rows = ranges * tokens // 2
    tp = lax.axis_index("tp")
    away[...] = total[
        pl.ds(pl.multiple_of((1 - tp) * half_rows, half_rows), half_rows), :
    ].astype(BF16)
    swap = pltpu.make_async_remote_copy(
        src_ref=away,
        dst_ref=arrived,
        send_sem=tp_sems.at[0],
        recv_sem=tp_sems.at[1],
        device_id={"tp": 1 - tp},
        device_id_type=MESH,
    )
    swap.start()
    ask.finish()
    tell.finish()
    for one in sent:
        one.wait_send()
    swap.wait()
    mine = total[pl.ds(pl.multiple_of(tp * half_rows, half_rows), half_rows), :]
    columns = total.shape[1]
    joined = mine + arrived[...].astype(F32)
    owners, size = ranges // 2, ranges // 2 * toks
    for c in range(columns // 128):
        lines[c, 0] = joined[:, c * 128 : (c + 1) * 128]
        for j in range(cands):
            for t in range(toks):
                lines[c, 1, pl.ds(j * size + t, owners, stride=toks), :] = lines[
                    c, 0, pl.ds(j * toks + t, owners, stride=tokens), :
                ]
            out_ref[j, :, c * 128 : (c + 1) * 128] = lines[
                c, 1, j * size : (j + 1) * size, :
            ].astype(BF16)


def on_device(
    queries,
    cand_keys,
    candidate_values,
    cached_prompt_keys,
    cached_prompt_values,
    block_lists,
    out_weight,
):
    cands, toks, heads, head = queries.shape
    kv = cand_keys.shape[2]
    group = heads // kv
    blocks, block_tokens = cached_prompt_keys.shape[:2]
    ranges = lax.axis_size("ctx")
    depth = ranges // 4
    piece = cands * toks * heads
    per = toks * group
    pair = kv // 2
    vmem = pl.BlockSpec(memory_space=pltpu.VMEM)
    anywhere = pl.BlockSpec(memory_space=pl.ANY)
    tile_owners = min(ranges, 256 // per)
    rows = tile_owners * per
    half_rows = piece // 2 + per
    most = min(blocks, cands * block_lists.shape[1] // ranges)
    entries = most + (cands - 1) * most // 2
    slots = ((entries + cands) // 2 + 1) // 2 * 2
    columns = out_weight.shape[1]
    tokens = cands * toks
    half = ranges * tokens // 2
    semaphores = [pltpu.SemaphoreType.DMA((4, depth, 2))] * 2
    block = pltpu.VMEM((depth, 2, half_rows, head), BF16)
    sizes = (cands, toks, kv, group, head, tile_owners, slots)
    cache = (blocks, block_tokens * kv, head)
    return pl.pallas_call(
        functools.partial(fused_kernel, ranges, sizes),
        out_shape=jax.ShapeDtypeStruct((cands, ranges * toks // 2, columns), BF16),
        in_specs=[pl.BlockSpec(memory_space=pltpu.SMEM)] + [vmem] * 4 + [anywhere] * 3,
        out_specs=vmem,
        scratch_shapes=[
            pltpu.VMEM((ranges, 2, cands, toks, heads // 2, head), BF16),
            pltpu.VMEM((2, *cache), BF16),
            pltpu.VMEM((block_tokens * kv, head), F32),
            pltpu.VMEM((2, kv, blocks, block_tokens, head), BF16),
            pltpu.SMEM((6, slots), jnp.int32),
            pltpu.VMEM((pair, cands, rows, head), BF16),
            pltpu.VMEM((2, kv, block_tokens, head), BF16),
            pltpu.VMEM((pair, slots, 2, rows, block_tokens), F32),
            pltpu.VMEM((pair, slots + 1, rows, block_tokens), F32),
            pltpu.VMEM((pair, slots + 1, rows, head), F32),
            pltpu.VMEM((pair, cands, rows, block_tokens), F32),
            pltpu.VMEM((pair, cands, rows, block_tokens), F32),
            pltpu.VMEM((pair, cands, rows, head), F32),
            pltpu.VMEM((ranges, 2, half_rows, head), BF16),
        ]
        + [block] * 6
        + [
            pltpu.VMEM((ranges, 2, piece // 2, head), BF16),
            pltpu.VMEM((piece, head), F32),
            pltpu.VMEM(out_weight.shape, BF16),
            pltpu.VMEM((2 * half, columns), F32),
            pltpu.VMEM((half, columns), BF16),
            pltpu.VMEM((half, columns), BF16),
            pltpu.VMEM((columns // 128, 2, half, 128), F32),
            pltpu.SemaphoreType.DMA((3,)),
            *semaphores,
            *semaphores,
            *semaphores,
            pltpu.SemaphoreType.DMA((2,)),
        ],
        compiler_params=pltpu.CompilerParams(
            collective_id=0, has_side_effects=True, vmem_limit_bytes=60 * 1024 * 1024
        ),
        name="verify",
    )(
        block_lists,
        block_lists,
        queries,
        cand_keys,
        candidate_values,
        cached_prompt_keys.reshape(cache),
        cached_prompt_values.reshape(cache),
        out_weight,
    )


def solution(mesh):
    placed = (
        P("groups", "ctx", "tp", None),
        P("groups", "ctx", "tp", None),
        P("groups", "ctx", "tp", None),
        P(("groups", "ctx"), None, "tp", None),
        P(("groups", "ctx"), None, "tp", None),
        P("groups", None),
        P("tp", "ctx"),
    )
    return jax.shard_map(
        on_device, mesh=mesh, in_specs=placed, out_specs=P("groups", "tp", "ctx"), check_vma=False
    )
```

time: 79.3 us -> 71.2 us (0.90)
  Pallas kernels: 76.9 us -> 69.5 us
    pallas_call x3 -> x1, Pallas kernels: 76.9 us -> 69.5 us  [on_device(): pl.pallas_call(functools.partial(fused_kernel, ranges, sizes), out_shape=...]
where the time goes in v1:
time: 71.2 us; the launch traced here: 71 us
  Pallas kernels  69.5 us (98%)
  local copies, waits for them, and re-layouts  1.47 us (2%)
    pallas_call x1, Pallas kernels, on_device(): pl.pallas_call(functools.partial(fused_kernel, ranges, sizes), out_shape=...  69.5 us
    unnamed x1, local copies, waits for them, and re-layouts  1.47 us

profile of v1, /device:TPU:0, one launch (start us, length us, event | category | flops | bytes accessed | tf_op | source)
XLA Modules:
  0.0 71.0 jit_solution(1167357988990944382)
XLA Ops:
  0.0 69.5 %verify.1 = bf16[4,16,512]{2,1,0:T(8,128)(2,1)} custom-call(s32[4,128]{1,0:T(4,128)} %lists_ref.1, s32[4,128]{1,0:T(4,128)} %lists_ref.1, bf16[4,2,32,128]{3,2,1,0:T(8,128)(2,1)} %q_ref.1, bf16[4,2,4,128]{3,2,1,0:T(4,128)(2,1)} %own_k_ref.1, bf16[4,2,4,128]{3,2,1,0:T(4,128)(2,1)} %own_v_ref.1, bf16[16,512,128]{2,1,0:T(8,128)(2,1)} %bitcast.2, ...), custom_call_target="tpu_custom_call" | custom-call | tf_op jit(solution)/shard_map/verify/pallas_call | solution.py:627
  69.5 1.5 %copy.9 = bf16[4,16,512]{2,1,0:T(8,128)(2,1)} copy(bf16[4,16,512]{2,1,0:T(8,128)(2,1)} %verify.1) | data formatting | bytes 131072

commit v2 on v1

--- a/solution.py
+++ b/solution.py
@@ -71,75 +71,56 @@
 class Gather:
     def __init__(self, place, buf, send, recv):
         self.place, self.buf, self.send, self.recv = place, buf, send, recv
-        self.sent = []
         self.z_of = [place.shifted(-d) for d in range(place.depth)]
 
-    def copy(self, kind, d, half, owner, target):
-        return pltpu.make_async_remote_copy(
-            src_ref=self.buf.at[owner, half],
-            dst_ref=self.buf.at[owner, half],
-            send_sem=self.send.at[kind, d, half],
-            recv_sem=self.recv.at[kind, d, half],
+    def go(self, piece, slot, half, target):
+        pltpu.make_async_remote_copy(
+            src_ref=piece,
+            dst_ref=piece,
+            send_sem=self.send,
+            recv_sem=self.recv.at[slot, half],
             device_id={"ctx": target},
             device_id_type=MESH,
-        )
-
-    def go(self, *what):
-        one = self.copy(*what)
-        one.start()
-        self.sent.append(one)
+        ).start()
+
+    def wait(self, count, slot, half):
+        some = self.buf.at[pl.ds(0, count), half]
+        pltpu.make_async_copy(some, some, self.recv.at[slot, half]).wait()
 
     def begin(self, half):
         place = self.place
         self.spread(0, half)
-        for d in near_first(place.depth):
-            self.go(0, d, half, place.me, place.line(d))
+        for d in near_first(place.depth)[::-1]:
+            self.go(self.buf.at[place.me, half], d, half, place.line(d))
 
     def spread(self, d, half):
         place = self.place
         owner = place.at(self.z_of[d], place.y, place.x)
         if d:
-            self.copy(0, d, half, owner, place.me).wait_recv()
-        self.go(1, d, half, owner, place.beside_x)
-        self.go(2, d, half, owner, place.beside_y)
+            self.wait(1, d, half)
+        for target in (place.beside_x, place.beside_y):
+            self.go(self.buf.at[owner, half], place.depth + d, half, target)
 
     def relay(self, d, half):
         place = self.place
-        if half == 0:
-            from_x = place.at(self.z_of[d], place.y, 1 - place.x)
-            self.copy(1, d, half, from_x, place.me).wait_recv()
-            self.go(3, d, half, from_x, place.beside_y)
-        else:
-            from_y = place.at(self.z_of[d], 1 - place.y, place.x)
-            self.copy(2, d, half, from_y, place.me).wait_recv()
-            self.go(3, d, half, from_y, place.beside_x)
+        self.wait(2, place.depth + d, half)
+        size = self.buf.shape[2] // 2
+        from_x = place.at(self.z_of[d], place.y, 1 - place.x)
+        from_y = place.at(self.z_of[d], 1 - place.y, place.x)
+        self.go(self.buf.at[from_x, half, pl.ds(0, size)], 0, half, place.beside_y)
+        self.go(self.buf.at[from_y, half, pl.ds(size, size)], 0, half, place.beside_x)
 
     def settle(self, half):
-        place = self.place
-        for d in range(place.depth):
-            from_x = place.at(self.z_of[d], place.y, 1 - place.x)
-            from_y = place.at(self.z_of[d], 1 - place.y, place.x)
-            if half == 0:
-                self.copy(2, d, half, from_y, place.me).wait_recv()
-            else:
-                self.copy(1, d, half, from_x, place.me).wait_recv()
-            across = place.at(self.z_of[d], 1 - place.y, 1 - place.x)
-            self.copy(3, d, half, across, place.me).wait_recv()
+        self.wait(self.place.depth, 0, half)
 
     def finish(self):
-        for one in self.sent:
-            one.wait_send()
+        away = self.buf.at[pl.ds(0, self.buf.shape[0] - 1)]
+        pltpu.make_async_copy(away, away, self.send).wait()
 
 
 def run_all(steps):
     for step in steps:
         step()
-
-
-def weave(first, second):
-    keyed = [((i + 0.5) / len(first), 0, i, step) for i, step in enumerate(first)]
-    keyed += [((i + 0.5) / len(second), 1, i, step) for i, step in enumerate(second)]
-    return [item[3] for item in sorted(keyed, key=lambda item: item[:3])]
 
 
 def fused_kernel(
@@ -195,7 +176,6 @@
     depth = place.depth
     per = toks * group
     pair = kv // 2
-    combos = pair * cands
     scale = head ** (-0.5) * math.log2(math.e)
     rows = tile_owners * per
     blocks, block_tokens = raw.shape[1], raw.shape[2] // kv
@@ -204,7 +184,6 @@
     for fetch in fetches:
         fetch.start()
     weight_fetch = pltpu.make_async_copy(weight_ref, weight, in_sems.at[2])
-    weight_fetch.start()
     for half in range(2):
         everyone[place.me, half] = q_ref[:, :, half * pair * group : (half + 1) * pair * group, :]
     greet(place, True)
@@ -274,25 +253,25 @@
 
         return step
 
-    def ask_steps(gather):
-        steps = []
-        pieces = [(d, half) for half in range(2) for d in [0] + near]
-        spreads = [piece for piece in pieces if piece[0]]
-        for i, piece in enumerate(pieces):
-            ahead = spreads[2 * i : 2 * i + 2] if i == 0 else spreads[i + 1 : i + 2]
-            for other in ahead:
-                steps.append(functools.partial(gather.spread, *other))
-            steps.append(functools.partial(gather.relay, *piece))
-        return steps
-
-    local = [sort_step(0, part) for part in range(4)] + [own_rows]
-    local += [sort_step(1, part) for part in range(4)]
-    run_all(weave(local, ask_steps(ask)))
+    part = functools.partial
+
+    def each(step, ds, half):
+        return [part(step, d, half) for d in ds]
+
+    come = near[::-1]
+    run_all([sort_step(0, i) for i in range(4)])
+    ask.relay(0, 0)
+    run_all(each(ask.spread, come[:1], 0) + [sort_step(1, 0)])
+    weight_fetch.start()
+    run_all(each(ask.spread, come[1:], 0) + [sort_step(1, 1)])
+    ask.relay(0, 1)
+    run_all(each(ask.spread, come, 1) + [sort_step(1, 2), sort_step(1, 3), own_rows])
+    run_all(each(ask.relay, come, 0))
 
     nt = (((1,), (1,)), ((), ()))
     row = lax.broadcasted_iota(jnp.int32, (rows, block_tokens), 0)
     lane = lax.broadcasted_iota(jnp.int32, (rows, block_tokens), 1)
-    unroll = 2
+    unroll = max(n for n in range(1, 12) if slots % n == 0)
 
     def attend(half, tile, between):
         owners = pl.ds(tile * tile_owners, tile_owners)
@@ -347,6 +326,7 @@
                     p.astype(BF16), own_blocks[1, h], preferred_element_type=F32
                 )
                 peaks[hh, j] = jnp.broadcast_to(peak, (rows, block_tokens))
+        between[1]()
 
         def second_pass(it, carry):
             for u in range(unroll):
@@ -366,46 +346,41 @@
                     )
             return carry
 
-        lax.fori_loop(0, slots // unroll, second_pass, 0)
-        between[1]()
+        middle = slots // unroll // 2
+        lax.fori_loop(0, middle, second_pass, 0)
+        between[2]()
+        lax.fori_loop(middle, slots // unroll, second_pass, 0)
+        between[3]()
         lanes = lax.broadcasted_iota(jnp.int32, (rows, 128), 1)
-        stats = jnp.zeros((rows, 128), F32)
         for hh in range(pair):
+            stats = jnp.zeros((rows, 128), F32)
             for j in range(cands):
-                combo = hh * cands + j
                 last, some = start[j + 1], count[j] > 0
                 sums = jnp.where(some, run[hh, last], 0.0) + own_sums[hh, j]
                 found = jnp.where(some, acc[hh, last], 0.0) + own_acc[hh, j]
-                stats = jnp.where(lanes == combo, peaks[hh, j], stats)
+                stats = jnp.where(lanes == j, peaks[hh, j], stats)
                 stats = jnp.where(
-                    lanes == 64 + combo, jnp.sum(sums, axis=1, keepdims=True), stats
+                    lanes == 64 + j, jnp.sum(sums, axis=1, keepdims=True), stats
                 )
-                parts_ref[owners, half, combo * per : (combo + 1) * per, :] = found.reshape(
+                parts_ref[owners, half, hh, j * per : (j + 1) * per, :] = found.reshape(
                     tile_owners, per, head
                 ).astype(BF16)
-        parts_ref[owners, half, combos * per : (combos + 1) * per, :] = stats.reshape(
-            tile_owners, per, 128
-        ).astype(BF16)
-
-    sent = []
-
-    def copy(kind, d, half, src, dst, target):
-        return pltpu.make_async_remote_copy(
+            parts_ref[owners, half, hh, cands * per : (cands + 1) * per, :] = stats.reshape(
+                tile_owners, per, 128
+            ).astype(BF16)
+
+    def go(slot, half, src, dst, target):
+        pltpu.make_async_remote_copy(
             src_ref=src,
-            dst_ref=dst.at[d, half],
-            send_sem=red_send.at[kind, d, half],
-            recv_sem=red_recv.at[kind, d, half],
+            dst_ref=dst,
+            send_sem=red_send,
+            recv_sem=red_recv.at[slot, half],
             device_id={"ctx": target},
             device_id_type=MESH,
-        )
-
-    def go(*what):
-        one = copy(*what)
-        one.start()
-        sent.append(one)
-
-    def arrive(kind, d, half, dst):
-        copy(kind, d, half, dst.at[d, half], dst, place.me).wait_recv()
+        ).start()
+
+    def arrive(slot, half, some):
+        pltpu.make_async_copy(some, some, red_recv.at[slot, half]).wait()
 
     def owner(d, flip_y, flip_x):
         y = 1 - place.y if flip_y else place.y
@@ -415,70 +390,66 @@
     def loader(ref, *index):
         return lambda start, size: ref[(*index, pl.ds(start, size), slice(None))]
 
-    def put(dst, d, half, sums, stats):
-        for c in range(combos):
-            dst[d, half, c * per : (c + 1) * per, :] = sums[c].astype(BF16)
-        dst[d, half, combos * per : (combos + 1) * per, :] = stats.astype(BF16)
+    def put(dst, index, sums, stats):
+        for c in range(cands):
+            dst[(*index, slice(c * per, (c + 1) * per), slice(None))] = sums[c].astype(BF16)
+        dst[(*index, slice(cands * per, (cands + 1) * per), slice(None))] = stats.astype(BF16)
 
     def hand_over(d, half):
-        across = parts_ref.at[owner(d, 1, 1), half]
-        if half == 0:
-            go(0, d, half, across, from_diag, place.beside_x)
-        else:
-            go(0, d, half, across, from_diag, place.beside_y)
+        across = owner(d, 1, 1)
+        for u, target in enumerate((place.beside_x, place.beside_y)):
+            go(d, half, parts_ref.at[across, half, u], from_diag.at[d, half, u], target)
 
     def hand_beside(d, half):
-        if half == 0:
-            go(1, d, half, parts_ref.at[owner(d, 0, 1), half], from_x, place.beside_x)
-        else:
-            go(2, d, half, parts_ref.at[owner(d, 1, 0), half], from_y, place.beside_y)
+        x_owner, y_owner = owner(d, 0, 1), owner(d, 1, 0)
+        slot = depth + d
+        go(slot, half, parts_ref.at[x_owner, half, 0], from_x.at[d, half, 0], place.beside_x)
+        go(slot, half, parts_ref.at[y_owner, half, 1], from_y.at[d, half, 1], place.beside_y)
 
     def pass_on(d, half):
-        arrive(0, d, half, from_diag)
-        mine = owner(d, 1, 0) if half == 0 else owner(d, 0, 1)
-        pieces = (loader(parts_ref, mine, half), loader(from_diag, d, half))
-        sums, stats, _ = merge(pieces, combos, per, scale)
-        put(to_diag, d, half, sums, stats)
-        if half == 0:
-            go(2, d, half, to_diag.at[d, half], from_y, place.beside_y)
-        else:
-            go(1, d, half, to_diag.at[d, half], from_x, place.beside_x)
+        arrive(d, half, from_diag.at[d, half])
+        for u in range(2):
+            mine = owner(d, 1, 0) if u == 0 else owner(d, 0, 1)
+            pieces = (loader(parts_ref, mine, half, u), loader(from_diag, d, half, u))
+            sums, stats, _ = merge(pieces, cands, per, scale)
+            put(to_diag, (d, half, u), sums, stats)
+            into, target = (from_y, place.beside_y) if u == 0 else (from_x, place.beside_x)
+            go(depth + d, half, to_diag.at[d, half, u], into.at[d, half, u], target)
 
     def plane(d, half):
-        arrive(1, d, half, from_x)
-        arrive(2, d, half, from_y)
-        pieces = (
-            loader(parts_ref, owner(d, 0, 0), half),
-            loader(from_x, d, half),
-            loader(from_y, d, half),
-        )
-        sums, stats, _ = merge(pieces, combos, per, scale)
-        put(to_line, d, half, sums, stats)
+        arrive(depth + d, half, parts_ref.at[pl.ds(0, 2), half])
+        for u in range(2):
+            pieces = (
+                loader(parts_ref, owner(d, 0, 0), half, u),
+                loader(from_x, d, half, u),
+                loader(from_y, d, half, u),
+            )
+            sums, stats, _ = merge(pieces, cands, per, scale)
+            put(to_line, (d, half, u), sums, stats)
         if d:
-            go(3, d, half, to_line.at[d, half], from_line, place.line(d))
+            go(2 * depth, half, to_line.at[d, half], from_line.at[d, half], place.line(d))
 
     far = near[::-1] + [0]
 
     def hand_all(half):
         for d in far:
             hand_over(d, half)
+        for d in far:
             hand_beside(d, half)
 
     tokens = cands * toks
 
     def conclude(half):
-        for d in range(1, depth):
-            arrive(3, d, half, from_line)
-        sums, _, denominator = merge(
-            [loader(to_line, 0, half)] + [loader(from_line, d, half) for d in range(1, depth)],
-            combos,
-            per,
-            scale,
-        )
-        denominator = pltpu.roll(denominator, 64, 1)
-        for c in range(combos):
-            at = (half * combos + c) * per
-            ordered[at : at + per, :] = sums[c] / denominator[:, c : c + 1]
+        arrive(2 * depth, half, from_line.at[pl.ds(0, depth - 1), half])
+        for u in range(2):
+            lines_in = [loader(from_line, d, half, u) for d in range(1, depth)]
+            sums, _, denominator = merge(
+                [loader(to_line, 0, half, u)] + lines_in, cands, per, scale
+            )
+            inverse = 1.0 / pltpu.roll(denominator, 64, 1)
+            for c in range(cands):
+                at = ((half * 2 + u) * cands + c) * per
+                ordered[at : at + per, :] = sums[c] * inverse[:, c : c + 1]
         for hh in range(pair):
             h = half * pair + hh
             block = [
@@ -506,54 +477,48 @@
         )
         return carry
 
-    part = functools.partial
-    nothing = lambda: None
     tiles = ranges // tile_owners
 
-    def attend_all(half, first, second):
+    def attend_all(half, *steps):
         for tile in range(tiles):
             last = tile == tiles - 1
-            attend(half, tile, (first if last else nothing, second if last else nothing))
+            attend(half, tile, [part(run_all, some if last else []) for some in steps])
 
     ask.settle(0)
-    attend_all(0, nothing, nothing)
+    attend_all(0, each(ask.relay, come, 1), [], [], [])
     hand_all(0)
     ask.settle(1)
     early = depth // 2
     attend_all(
         1,
-        lambda: run_all([part(pass_on, d, 0) for d in far[:early]]),
-        lambda: run_all(
-            [part(pass_on, d, 0) for d in far[early:]] + [part(plane, d, 0) for d in far[:early]]
-        ),
+        each(pass_on, far[:early], 0),
+        each(pass_on, far[early:], 0),
+        each(plane, far[:early], 0),
+        each(plane, far[early:], 0),
     )
     hand_all(1)
-    run_all([part(plane, d, 0) for d in far[early:]])
+    run_all(each(pass_on, far[:early], 1))
     conclude(0)
     tell.begin(0)
-    reduce_one = [part(pass_on, d, 1) for d in far[:2]]
-    for i, d in enumerate(far):
-        if i + 2 < depth:
-            reduce_one.append(part(pass_on, far[i + 2], 1))
-        reduce_one.append(part(plane, d, 1))
-    spread_zero = [part(tell.spread, d, 0) for d in near]
-    relay_zero = [part(tell.relay, d, 0) for d in [0] + near]
-    tell_zero = spread_zero[:2] + relay_zero[:1]
-    for i in range(2, len(near)):
-        tell_zero += [spread_zero[i], relay_zero[i - 1]]
-    tell_zero += relay_zero[len(near) - 1 :]
-    run_all(weave(reduce_one, tell_zero))
+    run_all(each(pass_on, far[early:], 1))
+    run_all(each(plane, far, 1))
+    run_all(each(tell.relay, [0], 0) + each(tell.spread, come, 0))
     conclude(1)
     tell.begin(1)
     total[...] = jnp.zeros_like(total)
+    weight_fetch.wait()
+    run_all(each(tell.relay, come, 0))
+    count_half = kv * group // 4
     tell.settle(0)
-    weight_fetch.wait()
-    count_half = kv * group // 4
-    lax.fori_loop(0, count_half, project, 0)
-    for i, d in enumerate([0] + near):
-        for other in near[:2] if i == 0 else near[i + 1 : i + 2]:
-            tell.spread(other, 1)
-        tell.relay(d, 1)
+
+    def project_some(index, of):
+        lax.fori_loop(index * count_half // of, (index + 1) * count_half // of, project, 0)
+
+    run_all(each(tell.relay, [0], 1) + each(tell.spread, come[:-1], 1))
+    project_some(0, 2)
+    run_all(each(tell.spread, come[-1:], 1))
+    project_some(1, 2)
+    run_all(each(tell.relay, come, 1))
     tell.settle(1)
     lax.fori_loop(count_half, 2 * count_half, project, 0)
     half_rows = ranges * tokens // 2
@@ -572,8 +537,8 @@
     swap.start()
     ask.finish()
     tell.finish()
-    for one in sent:
-        one.wait_send()
+    handed = parts_ref.at[pl.ds(0, ranges - 1)]
+    pltpu.make_async_copy(handed, handed, red_send).wait()
     swap.wait()
     mine = total[pl.ds(pl.multiple_of(tp * half_rows, half_rows), half_rows), :]
     columns = total.shape[1]
@@ -613,15 +578,16 @@
     anywhere = pl.BlockSpec(memory_space=pl.ANY)
     tile_owners = min(ranges, 256 // per)
     rows = tile_owners * per
-    half_rows = piece // 2 + per
+    unit_rows = cands * per + per
     most = min(blocks, cands * block_lists.shape[1] // ranges)
     entries = most + (cands - 1) * most // 2
     slots = ((entries + cands) // 2 + 1) // 2 * 2
     columns = out_weight.shape[1]
     tokens = cands * toks
     half = ranges * tokens // 2
-    semaphores = [pltpu.SemaphoreType.DMA((4, depth, 2))] * 2
-    block = pltpu.VMEM((depth, 2, half_rows, head), BF16)
+    dma = pltpu.SemaphoreType.DMA
+    semaphores = lambda slots: [dma, dma((slots, 2))]
+    block = pltpu.VMEM((depth, 2, pair, unit_rows, head), BF16)
     sizes = (cands, toks, kv, group, head, tile_owners, slots)
     cache = (blocks, block_tokens * kv, head)
     return pl.pallas_call(
@@ -643,7 +609,7 @@
             pltpu.VMEM((pair, cands, rows, block_tokens), F32),
             pltpu.VMEM((pair, cands, rows, block_tokens), F32),
             pltpu.VMEM((pair, cands, rows, head), F32),
-            pltpu.VMEM((ranges, 2, half_rows, head), BF16),
+            pltpu.VMEM((ranges, 2, pair, unit_rows, head), BF16),
         ]
         + [block] * 6
         + [
@@ -655,9 +621,9 @@
             pltpu.VMEM((half, columns), BF16),
             pltpu.VMEM((columns // 128, 2, half, 128), F32),
             pltpu.SemaphoreType.DMA((3,)),
-            *semaphores,
-            *semaphores,
-            *semaphores,
+            *semaphores(2 * depth),
+            *semaphores(2 * depth + 1),
+            *semaphores(2 * depth),
             pltpu.SemaphoreType.DMA((2,)),
         ],
         compiler_params=pltpu.CompilerParams(

time: 71.2 us -> 62 us (0.87)
  Pallas kernels: 69.5 us -> 60.4 us
    pallas_call x1, Pallas kernels: 69.5 us -> 60.4 us  [on_device(): pl.pallas_call(functools.partial(fused_kernel, ranges, sizes), out_shape=...]
where the time goes in v2:
time: 62 us; the launch traced here: 61.8 us
  Pallas kernels  60.4 us (97%)
  local copies, waits for them, and re-layouts  1.47 us (2%)
    pallas_call x1, Pallas kernels, on_device(): pl.pallas_call(functools.partial(fused_kernel, ranges, sizes), out_shape=...  60.4 us
    unnamed x1, local copies, waits for them, and re-layouts  1.47 us

profile of v2, /device:TPU:0, one launch (start us, length us, event | category | flops | bytes accessed | tf_op | source)
XLA Modules:
  0.0 61.8 jit_solution(1171078108667917603)
XLA Ops:
  0.0 60.4 %verify.1 = bf16[4,16,512]{2,1,0:T(8,128)(2,1)} custom-call(s32[4,128]{1,0:T(4,128)} %lists_ref.1, s32[4,128]{1,0:T(4,128)} %lists_ref.1, bf16[4,2,32,128]{3,2,1,0:T(8,128)(2,1)} %q_ref.1, bf16[4,2,4,128]{3,2,1,0:T(4,128)(2,1)} %own_k_ref.1, bf16[4,2,4,128]{3,2,1,0:T(4,128)(2,1)} %own_v_ref.1, bf16[16,512,128]{2,1,0:T(8,128)(2,1)} %bitcast.2, ...), custom_call_target="tpu_custom_call" | custom-call | tf_op jit(solution)/shard_map/verify/pallas_call | solution.py:593
  60.4 1.5 %copy.9 = bf16[4,16,512]{2,1,0:T(8,128)(2,1)} copy(bf16[4,16,512]{2,1,0:T(8,128)(2,1)} %verify.1) | data formatting | bytes 131072

commit v3 on v2

--- a/solution.py
+++ b/solution.py
@@ -31,16 +31,14 @@
         return self.at(self.shifted(d), self.y, self.x)
 
 
-def greet(place, with_tp):
+def greet(place):
     barrier = pltpu.get_barrier_semaphore()
     others = [place.line(d) for d in range(1, place.depth)]
     for other in others + [place.beside_x, place.beside_y]:
         pl.semaphore_signal(barrier, inc=1, device_id={"ctx": other}, device_id_type=MESH)
-    if with_tp:
-        pl.semaphore_signal(
-            barrier, inc=1, device_id={"tp": 1 - lax.axis_index("tp")}, device_id_type=MESH
-        )
-    pl.semaphore_wait(barrier, place.depth + 1 + int(with_tp))
+    pl.semaphore_signal(
+        barrier, inc=1, device_id={"tp": 1 - lax.axis_index("tp")}, device_id_type=MESH
+    )
 
 
 def near_first(depth):
@@ -90,7 +88,7 @@
     def begin(self, half):
         place = self.place
         self.spread(0, half)
-        for d in near_first(place.depth)[::-1]:
+        for d in near_first(place.depth):
             self.go(self.buf.at[place.me, half], d, half, place.line(d))
 
     def spread(self, d, half):
@@ -127,14 +125,17 @@
     ranges,
     sizes,
     lists_smem,
-    lists_ref,
+    lists_hbm,
     q_ref,
-    own_k_ref,
-    own_v_ref,
+    own_k_hbm,
+    own_v_hbm,
     k_ref,
     v_ref,
     weight_ref,
     out_ref,
+    lists_ref,
+    own_k_ref,
+    own_v_ref,
     everyone,
     raw,
     wide,
@@ -179,19 +180,36 @@
     scale = head ** (-0.5) * math.log2(math.e)
     rows = tile_owners * per
     blocks, block_tokens = raw.shape[1], raw.shape[2] // kv
+    greet(place)
+    mine = [
+        pltpu.make_async_copy(
+            q_ref.at[:, :, pl.ds(half * pair * group, pair * group), :],
+            everyone.at[place.me, half],
+            in_sems.at[3],
+        )
+        for half in range(2)
+    ]
+    small = [(lists_hbm, lists_ref), (own_k_hbm, own_k_ref), (own_v_hbm, own_v_ref)]
+    local = [
+        pltpu.make_async_copy(src, dst, in_sems.at[4 + n]) for n, (src, dst) in enumerate(small)
+    ]
+    for one in mine + local:
+        one.start()
     sources = (k_ref, v_ref)
     fetches = [pltpu.make_async_copy(sources[n], raw.at[n], in_sems.at[n]) for n in range(2)]
     for fetch in fetches:
         fetch.start()
     weight_fetch = pltpu.make_async_copy(weight_ref, weight, in_sems.at[2])
-    for half in range(2):
-        everyone[place.me, half] = q_ref[:, :, half * pair * group : (half + 1) * pair * group, :]
-    greet(place, True)
+    whole = everyone.at[place.me]
+    pltpu.make_async_copy(whole, whole, in_sems.at[3]).wait()
+    pl.semaphore_wait(pltpu.get_barrier_semaphore(), depth + 2)
 
     ask = Gather(place, everyone, ask_send, ask_recv)
     near = near_first(depth)
     ask.begin(0)
     ask.begin(1)
+    for one in local:
+        one.wait()
 
     lowest = place.me * blocks
     listed = lists_smem.shape[1]
@@ -258,7 +276,7 @@
     def each(step, ds, half):
         return [part(step, d, half) for d in ds]
 
-    come = near[::-1]
+    come = near
     run_all([sort_step(0, i) for i in range(4)])
     ask.relay(0, 0)
     run_all(each(ask.spread, come[:1], 0) + [sort_step(1, 0)])
@@ -463,16 +481,19 @@
 
     tell = Gather(place, gathered, send, recv)
 
+    count_half = kv * group // 2
+    deep = math.gcd(count_half, 8)
+
     def project(i, carry):
-        steps = kv * group // 4
-        start_row = pl.multiple_of((i % steps) * 2 * tokens, 2 * tokens)
-        both = gathered[:, i // steps, pl.ds(start_row, 2 * tokens), :].astype(F32)
-        left = both[:, :tokens, :].reshape(ranges * tokens, head).astype(BF16)
-        right = both[:, tokens:, :].reshape(ranges * tokens, head).astype(BF16)
-        rows_at = pl.multiple_of(i * 2 * head, 2 * head)
+        at = pl.multiple_of((i * deep) % count_half * tokens, deep * tokens)
+        some = gathered[:, i * deep // count_half, pl.ds(at, deep * tokens), :].astype(F32)
+        inputs = [
+            some[:, n * tokens : (n + 1) * tokens, :].reshape(ranges * tokens, head).astype(BF16)
+            for n in range(deep)
+        ]
         total[...] += jnp.dot(
-            jnp.concatenate([left, right], axis=1),
-            weight[pl.ds(rows_at, 2 * head), :],
+            jnp.concatenate(inputs, axis=1),
+            weight[pl.ds(pl.multiple_of(i * deep * head, deep * head), deep * head), :],
             preferred_element_type=F32,
         )
         return carry
@@ -493,34 +514,26 @@
         1,
         each(pass_on, far[:early], 0),
         each(pass_on, far[early:], 0),
-        each(plane, far[:early], 0),
-        each(plane, far[early:], 0),
+        [],
+        each(plane, far, 0),
     )
     hand_all(1)
-    run_all(each(pass_on, far[:early], 1))
+    run_all(each(pass_on, far, 1))
     conclude(0)
+    run_all(each(plane, far, 1))
     tell.begin(0)
-    run_all(each(pass_on, far[early:], 1))
-    run_all(each(plane, far, 1))
-    run_all(each(tell.relay, [0], 0) + each(tell.spread, come, 0))
     conclude(1)
     tell.begin(1)
     total[...] = jnp.zeros_like(total)
     weight_fetch.wait()
-    run_all(each(tell.relay, come, 0))
-    count_half = kv * group // 4
+    run_all(each(tell.relay, [0], 0) + each(tell.spread, come, 0))
+    run_all(each(tell.relay, [0], 1) + each(tell.spread, come, 1))
+    run_all(each(tell.relay, come, 0) + each(tell.relay, come, 1))
+    steps = count_half // deep
     tell.settle(0)
-
-    def project_some(index, of):
-        lax.fori_loop(index * count_half // of, (index + 1) * count_half // of, project, 0)
-
-    run_all(each(tell.relay, [0], 1) + each(tell.spread, come[:-1], 1))
-    project_some(0, 2)
-    run_all(each(tell.spread, come[-1:], 1))
-    project_some(1, 2)
-    run_all(each(tell.relay, come, 1))
+    lax.fori_loop(0, steps, project, 0)
     tell.settle(1)
-    lax.fori_loop(count_half, 2 * count_half, project, 0)
+    lax.fori_loop(steps, 2 * steps, project, 0)
     half_rows = ranges * tokens // 2
     tp = lax.axis_index("tp")
     away[...] = total[
@@ -593,9 +606,12 @@
     return pl.pallas_call(
         functools.partial(fused_kernel, ranges, sizes),
         out_shape=jax.ShapeDtypeStruct((cands, ranges * toks // 2, columns), BF16),
-        in_specs=[pl.BlockSpec(memory_space=pltpu.SMEM)] + [vmem] * 4 + [anywhere] * 3,
+        in_specs=[pl.BlockSpec(memory_space=pltpu.SMEM)] + [anywhere] * 7,
         out_specs=vmem,
         scratch_shapes=[
+            pltpu.VMEM(block_lists.shape, jnp.int32),
+            pltpu.VMEM(cand_keys.shape, BF16),
+            pltpu.VMEM(candidate_values.shape, BF16),
             pltpu.VMEM((ranges, 2, cands, toks, heads // 2, head), BF16),
             pltpu.VMEM((2, *cache), BF16),
             pltpu.VMEM((block_tokens * kv, head), F32),
@@ -620,11 +636,11 @@
             pltpu.VMEM((half, columns), BF16),
             pltpu.VMEM((half, columns), BF16),
             pltpu.VMEM((columns // 128, 2, half, 128), F32),
-            pltpu.SemaphoreType.DMA((3,)),
+            dma((7,)),
             *semaphores(2 * depth),
             *semaphores(2 * depth + 1),
             *semaphores(2 * depth),
-            pltpu.SemaphoreType.DMA((2,)),
+            dma((2,)),
         ],
         compiler_params=pltpu.CompilerParams(
             collective_id=0, has_side_effects=True, vmem_limit_bytes=60 * 1024 * 1024

time: 62 us -> 59 us (0.952)
  Pallas kernels: 60.4 us -> 57.3 us
    pallas_call x1, Pallas kernels: 60.4 us -> 57.3 us  [on_device(): pl.pallas_call(functools.partial(fused_kernel, ranges, sizes), out_shape=...]
where the time goes in v3:
time: 59 us; the launch traced here: 58.8 us
  Pallas kernels  57.3 us (97%)
  local copies, waits for them, and re-layouts  1.47 us (2%)
    pallas_call x1, Pallas kernels, on_device(): pl.pallas_call(functools.partial(fused_kernel, ranges, sizes), out_shape=...  57.3 us
    unnamed x1, local copies, waits for them, and re-layouts  1.47 us

profile of v3, /device:TPU:0, one launch (start us, length us, event | category | flops | bytes accessed | tf_op | source)
XLA Modules:
  0.0 58.8 jit_solution(8837556059803313109)
XLA Ops:
  0.0 57.3 %verify.1 = bf16[4,16,512]{2,1,0:T(8,128)(2,1)} custom-call(s32[4,128]{1,0:T(4,128)} %lists_hbm.1, s32[4,128]{1,0:T(4,128)} %lists_hbm.1, bf16[4,2,32,128]{3,2,1,0:T(8,128)(2,1)} %q_ref.1, bf16[4,2,4,128]{3,2,1,0:T(4,128)(2,1)} %own_k_hbm.1, bf16[4,2,4,128]{3,2,1,0:T(4,128)(2,1)} %own_v_hbm.1, bf16[16,512,128]{2,1,0:T(8,128)(2,1)} %bitcast.2, ...), custom_call_target="tpu_custom_call" | custom-call | tf_op jit(solution)/shard_map/verify/pallas_call | solution.py:606
  57.3 1.5 %copy.9 = bf16[4,16,512]{2,1,0:T(8,128)(2,1)} copy(bf16[4,16,512]{2,1,0:T(8,128)(2,1)} %verify.1) | data formatting | bytes 131072

commit v4 on v3

--- a/solution.py
+++ b/solution.py
@@ -515,9 +515,10 @@
         each(pass_on, far[:early], 0),
         each(pass_on, far[early:], 0),
         [],
-        each(plane, far, 0),
+        each(plane, far[:early], 0),
     )
     hand_all(1)
+    run_all(each(plane, far[early:], 0))
     run_all(each(pass_on, far, 1))
     conclude(0)
     run_all(each(plane, far, 1))

time: 59 us -> 58 us (0.983)
  Pallas kernels: 57.3 us -> 56.4 us
    pallas_call x1, Pallas kernels: 57.3 us -> 56.4 us  [on_device(): pl.pallas_call(functools.partial(fused_kernel, ranges, sizes), out_shape=...]
where the time goes in v4:
time: 58 us; the launch traced here: 57.8 us
  Pallas kernels  56.4 us (97%)
  local copies, waits for them, and re-layouts  1.47 us (3%)
    pallas_call x1, Pallas kernels, on_device(): pl.pallas_call(functools.partial(fused_kernel, ranges, sizes), out_shape=...  56.4 us
    unnamed x1, local copies, waits for them, and re-layouts  1.47 us

profile of v4, /device:TPU:0, one launch (start us, length us, event | category | flops | bytes accessed | tf_op | source)
XLA Modules:
  0.0 57.8 jit_solution(628780824952861550)
XLA Ops:
  0.0 56.4 %verify.1 = bf16[4,16,512]{2,1,0:T(8,128)(2,1)} custom-call(s32[4,128]{1,0:T(4,128)} %lists_hbm.1, s32[4,128]{1,0:T(4,128)} %lists_hbm.1, bf16[4,2,32,128]{3,2,1,0:T(8,128)(2,1)} %q_ref.1, bf16[4,2,4,128]{3,2,1,0:T(4,128)(2,1)} %own_k_hbm.1, bf16[4,2,4,128]{3,2,1,0:T(4,128)(2,1)} %own_v_hbm.1, bf16[16,512,128]{2,1,0:T(8,128)(2,1)} %bitcast.2, ...), custom_call_target="tpu_custom_call" | custom-call | tf_op jit(solution)/shard_map/verify/pallas_call | solution.py:607
  56.4 1.5 %copy.9 = bf16[4,16,512]{2,1,0:T(8,128)(2,1)} copy(bf16[4,16,512]{2,1,0:T(8,128)(2,1)} %verify.1) | data formatting | bytes 131072
